TPU v7x, 128 devices: a whole 4x4x4 slice. The times are simulated.
128 devices in a mesh: gx: 8 (over y_lo, z), gy: 16 (over y_hi, x, core).
Axes of the slice: x: 4, y: 4 (y_hi: 2, y_lo: 2; y = y_hi * 2 + y_lo), z: 4, core: 2. Of those that a mesh axis runs over, the one named last changes fastest.
Arguments:
- thickness: float32 [4096, 2048], P('gy', 'gx'), may hold values from 0.5 to 2
- driving: float32 [2, 4096, 2048], P(None, 'gy', 'gx'), may hold values from -6 to 6
- observed: float32 [2, 4096, 2048], P(None, 'gy', 'gx'), may hold values from -2 to 2
- control: float32 [64, 4096], P('gy'), may hold values from 0.5 to 1.5
- ice_mask: int32 [16, 8], replicated, may hold values 0 or 1
- tile_block: int32 [16, 8, 1], replicated, may hold values from 0 to 63
Outputs:
- vel_u: float32 [4096, 2048], P('gy', 'gx')
- vel_v: float32 [4096, 2048], P('gy', 'gx')
- grad_control: float32 [64, 4096], P('gy')
Inputs may be any that keep to these rules, and one draw needn't show every extreme that they name: `tile_block`: every one of the 64 control blocks is named by at least one tile.
All inputs are finite; a program needn't handle non-finite values.
Results may differ from a plain program's by a relative error of at most 0.00015.
Values sent between devices are 32-bit elements; how exact they have to be, the bound alone decides.
A program may use at most 64 MiB of HBM per device.

v0:
```python
import jax
import jax.numpy as jnp
from jax import lax
from jax.sharding import PartitionSpec as P

TILE = 256
CPC = 4
PIC = 4
SW = 2
ADJ = 6
CT = 64
COARSE = 4096
visc_scale = 0.1
strain_floor = 0.05


def with_halo(cells, sides, width):
    for axis, dim in sides:
        count = lax.axis_size(axis)
        ends = count - 1
        head = lax.slice_in_dim(cells, 0, width, axis=dim)
        tail = lax.slice_in_dim(cells, cells.shape[dim] - width, cells.shape[dim], axis=dim)
        cells = jnp.concatenate(
            [
                lax.ppermute(tail, axis, [(i, (i + 1) % count) for i in range(ends)]),
                cells,
                lax.ppermute(head, axis, [((i + 1) % count, i) for i in range(ends)]),
            ],
            axis=dim,
        )
    return cells


def viscosity(vel_pad, thick):
    speed_x = vel_pad[0]
    speed_y = vel_pad[1]
    dudx = 0.5 * (speed_x[1:-1, 2:] - speed_x[1:-1, :-2])
    dudy = 0.5 * (speed_x[2:, 1:-1] - speed_x[:-2, 1:-1])
    dvdx = 0.5 * (speed_y[1:-1, 2:] - speed_y[1:-1, :-2])
    dvdy = 0.5 * (speed_y[2:, 1:-1] - speed_y[:-2, 1:-1])
    shear = dudy + dvdx
    strain = dudx * dudx + dvdy * dvdy + dudx * dvdy + 0.25 * shear * shear + strain_floor
    return visc_scale * thick * jnp.power(strain, -1.0 / 3.0)


def coefficients(visc_pad, friction):
    center = visc_pad[1:-1, 1:-1]
    east_w = 0.5 * (center + visc_pad[1:-1, 2:])
    west_w = 0.5 * (center + visc_pad[1:-1, :-2])
    south_w = 0.5 * (center + visc_pad[2:, 1:-1])
    north_w = 0.5 * (center + visc_pad[:-2, 1:-1])
    diag_u = friction + 4.0 * (east_w + west_w) + south_w + north_w
    diag_v = friction + east_w + west_w + 4.0 * (south_w + north_w)
    return (visc_pad, east_w, west_w, south_w, north_w, diag_u, diag_v)


def relaxation(vel_pad, stencil_coef, forcing, ice_cells):
    visc_pad, east_w, west_w, south_w, north_w, diag_u, diag_v = stencil_coef
    speed_x = vel_pad[0]
    speed_y = vel_pad[1]
    flux_p = 2.0 * visc_pad[1:-1, :] * (0.5 * (speed_y[2:, :] - speed_y[:-2, :]))
    flux_q = visc_pad[:, 1:-1] * (0.5 * (speed_y[:, 2:] - speed_y[:, :-2]))
    cross_u = 0.5 * (flux_p[:, 2:] - flux_p[:, :-2]) + 0.5 * (flux_q[2:, :] - flux_q[:-2, :])
    flux_r = 2.0 * visc_pad[:, 1:-1] * (0.5 * (speed_x[:, 2:] - speed_x[:, :-2]))
    flux_s = visc_pad[1:-1, :] * (0.5 * (speed_x[2:, :] - speed_x[:-2, :]))
    cross_v = 0.5 * (flux_r[2:, :] - flux_r[:-2, :]) + 0.5 * (flux_s[:, 2:] - flux_s[:, :-2])
    near_u = (
        4.0 * (east_w * speed_x[1:-1, 2:] + west_w * speed_x[1:-1, :-2])
        + south_w * speed_x[2:, 1:-1]
        + north_w * speed_x[:-2, 1:-1]
    )
    near_v = (
        east_w * speed_y[1:-1, 2:]
        + west_w * speed_y[1:-1, :-2]
        + 4.0 * (south_w * speed_y[2:, 1:-1] + north_w * speed_y[:-2, 1:-1])
    )
    new_u = ice_cells * (forcing[0] + near_u + cross_u) / diag_u
    new_v = ice_cells * (forcing[1] + near_v + cross_v) / diag_v
    return jnp.stack([new_u, new_v])


def halo_velocity(field):
    return with_halo(field, (("gx", 2), ("gy", 1)), 1)


def per_device(thickness, driving, observed, control, ice_mask, tile_block):
    row_count, col_count = thickness.shape
    tile_count = col_count // TILE
    owned_rows = control.shape[0]
    row_tile = lax.axis_index("gy")
    col_tile = lax.axis_index("gx") * tile_count
    blocks = lax.dynamic_slice(tile_block[:, :, 0], (row_tile, col_tile), (1, tile_count))[0]
    ice_tiles = lax.dynamic_slice(ice_mask, (row_tile, col_tile), (1, tile_count))[0].astype(
        jnp.float32
    )
    ice_cells = jnp.broadcast_to(ice_tiles[None, :, None], (TILE, tile_count, TILE)).reshape(
        row_count, col_count
    )
    rates = jnp.exp(control)
    shard_rows = lax.all_gather(rates, "gy", axis=0, tiled=True)
    labels = jnp.arange(shard_rows.shape[0], dtype=jnp.int32)
    onehot = (blocks[:, None] == labels[None, :]).astype(jnp.float32)
    picked = jnp.dot(onehot, shard_rows, precision=lax.Precision.HIGHEST)
    friction = jnp.broadcast_to(
        picked.reshape(tile_count, CT, 1, CT, 1), (tile_count, CT, CPC, CT, CPC)
    )
    friction = (
        friction.reshape(tile_count, TILE, TILE).transpose(1, 0, 2).reshape(row_count, col_count)
    )
    velocity = jnp.zeros((2, row_count, col_count), jnp.float32)
    stencil_coef = None
    for picard in range(PIC):
        vel_pad = halo_velocity(velocity)
        visc_cells = viscosity(vel_pad, thickness)
        visc_pad = with_halo(visc_cells, (("gx", 1), ("gy", 0)), 1)
        stencil_coef = coefficients(visc_pad, friction)
        for sweep in range(SW):
            if sweep > 0:
                vel_pad = halo_velocity(velocity)
            velocity = relaxation(vel_pad, stencil_coef, driving, ice_cells)
    misfit = ice_cells * (velocity - observed)
    adjoint = jnp.zeros((2, row_count, col_count), jnp.float32)
    for sweep in range(ADJ):
        adjoint = relaxation(halo_velocity(adjoint), stencil_coef, misfit, ice_cells)
    cell_grad = -friction * (velocity[0] * adjoint[0] + velocity[1] * adjoint[1])
    tile_grad = cell_grad.reshape(CT, CPC, tile_count, CT, CPC).sum(axis=(1, 4))
    tile_grad = tile_grad.transpose(1, 0, 2).reshape(tile_count, COARSE)
    labels = jnp.arange(owned_rows * lax.axis_size("gy"), dtype=jnp.int32)
    onehot = (labels[:, None] == blocks[None, :]).astype(jnp.float32)
    partial_sum = lax.psum_scatter(
        jnp.dot(onehot, tile_grad, precision=lax.Precision.HIGHEST),
        "gy",
        scatter_dimension=0,
        tiled=True,
    )
    gradient = lax.psum(partial_sum, "gx")
    return (velocity[0], velocity[1], gradient)


def solution(mesh):
    return jax.shard_map(
        per_device,
        mesh=mesh,
        in_specs=(P("gy", "gx"), P(None, "gy", "gx"), P(None, "gy", "gx"), P("gy", None), P(), P()),
        out_specs=(P("gy", "gx"), P("gy", "gx"), P("gy", None)),
        check_vma=False,
    )
```

profile of v0, /device:TPU:0, one launch (start us, length us, event | category | flops | bytes accessed | tf_op | source)
XLA Modules:
  0.0 709.3 jit_solution(17794844136733789249)
XLA Ops:
  8.6 4.6 collective-permute-start
  26.5 5.0 collective-permute-start.5
  44.4 19.9 %all-gather.3.cloned.1.call-done = f32[16,4,4096]{2,1,0:T(4,128)} async-done(((f32[1,4,4096]{2,1,0:T(4,128)}), f32[16,4,4096]{2,1,0:T(4,128)}) %all-gather.3.cloned.1.call-update) | async-done | bytes 1048592 | tf_op jit(solution)/shard_map/all_gather | solution.py:100
  78.0 8.4 %broadcast_in_dim.8 = f32[256,256]{1,0:T(8,128)S(1)} reshape(f32[64,4,64,4]{3,2,1,0:T(8,128)} %broadcast_in_dim.7) | data formatting | bytes 524288 | tf_op jit(solution)/shard_map/broadcast_in_dim | solution.py:104
  90.5 4.7 collective-permute-start.8
  110.1 5.2 collective-permute-start.12
  115.3 5.0 collective-permute-done.13
  129.5 5.0 collective-permute-start.17
  146.9 5.0 collective-permute-start.20
  167.4 6.2 collective-permute-start.24
  187.6 7.1 %collective-permute-start.29 = (f32[256,1]{1,0:T(8,128)S(1)}, f32[256,1]{1,0:T(8,128)S(1)}, u32[]{:S(2)}, u32[]{:S(2)}) collective-permute-start(f32[256,1]{1,0:T(8,128)S(1)} %get-tuple-element.142), channel_id=1, source_target_pairs={{0,16},{16,32},{32,48},{48,64},{64,80},{80,96},{96,112},{1,17},{17... | collective-permute-start | bytes 3080 | tf_op jit(solution)/shard_map/ppermute | solution.py:25
  206.9 7.1 %collective-permute-start.32 = (f32[2,256,1]{2,1,0:T(8,128)S(1)}, f32[2,256,1]{2,1,0:T(8,128)S(1)}, u32[]{:S(2)}, u32[]{:S(2)}) collective-permute-start(f32[2,256,1]{2,1,0:T(8,128)S(1)} %get-tuple-element.99), channel_id=1, source_target_pairs={{0,16},{16,32},{32,48},{48,64},{64,80},{80,96},{96,112},{1,17},{17... | collective-permute-start | bytes 6152 | tf_op jit(solution)/shard_map/ppermute | solution.py:25
  219.9 4.8 collective-permute-start.34
  229.5 7.1 %collective-permute-start.36 = (f32[2,256,1]{2,1,0:T(8,128)S(1)}, f32[2,256,1]{2,1,0:T(8,128)S(1)}, u32[]{:S(2)}, u32[]{:S(2)}) collective-permute-start(f32[2,256,1]{2,1,0:T(8,128)S(1)} %get-tuple-element.97), channel_id=1, source_target_pairs={{0,16},{16,32},{32,48},{48,64},{64,80},{80,96},{96,112},{1,17},{17... | collective-permute-start | bytes 6152 | tf_op jit(solution)/shard_map/ppermute | solution.py:25
  241.9 5.5 collective-permute-start.38
  250.6 7.1 %collective-permute-start.41 = (f32[256,1]{1,0:T(8,128)S(1)}, f32[256,1]{1,0:T(8,128)S(1)}, u32[]{:S(2)}, u32[]{:S(2)}) collective-permute-start(f32[256,1]{1,0:T(8,128)S(1)} %get-tuple-element.140), channel_id=1, source_target_pairs={{0,16},{16,32},{32,48},{48,64},{64,80},{80,96},{96,112},{1,17},{17... | collective-permute-start | bytes 3080 | tf_op jit(solution)/shard_map/ppermute | solution.py:25
  262.1 5.2 collective-permute-start.43
  271.0 7.1 %collective-permute-start.44 = (f32[2,256,1]{2,1,0:T(8,128)S(1)}, f32[2,256,1]{2,1,0:T(8,128)S(1)}, u32[]{:S(2)}, u32[]{:S(2)}) collective-permute-start(f32[2,256,1]{2,1,0:T(8,128)S(1)} %get-tuple-element.95), channel_id=1, source_target_pairs={{0,16},{16,32},{32,48},{48,64},{64,80},{80,96},{96,112},{1,17},{17... | collective-permute-start | bytes 6152 | tf_op jit(solution)/shard_map/ppermute | solution.py:25
  284.1 5.2 collective-permute-start.46
  295.4 7.1 %collective-permute-start.48 = (f32[2,256,1]{2,1,0:T(8,128)S(1)}, f32[2,256,1]{2,1,0:T(8,128)S(1)}, u32[]{:S(2)}, u32[]{:S(2)}) collective-permute-start(f32[2,256,1]{2,1,0:T(8,128)S(1)} %get-tuple-element.93), channel_id=1, source_target_pairs={{0,16},{16,32},{32,48},{48,64},{64,80},{80,96},{96,112},{1,17},{17... | collective-permute-start | bytes 6152 | tf_op jit(solution)/shard_map/ppermute | solution.py:25
  308.5 4.8 collective-permute-start.50
  317.9 7.1 %collective-permute-start.52 = (f32[2,256,1]{2,1,0:T(8,128)S(1)}, f32[2,256,1]{2,1,0:T(8,128)S(1)}, u32[]{:S(2)}, u32[]{:S(2)}) collective-permute-start(f32[2,256,1]{2,1,0:T(8,128)S(1)} %get-tuple-element.91), channel_id=1, source_target_pairs={{0,16},{16,32},{32,48},{48,64},{64,80},{80,96},{96,112},{1,17},{17... | collective-permute-start | bytes 6152 | tf_op jit(solution)/shard_map/ppermute | solution.py:25
  340.3 6.8 collective-permute-start.56
  352.3 6.1 collective-permute-start.58
  363.0 7.1 %collective-permute-start.60 = (f32[2,256,1]{2,1,0:T(8,128)S(1)}, f32[2,256,1]{2,1,0:T(8,128)S(1)}, u32[]{:S(2)}, u32[]{:S(2)}) collective-permute-start(f32[2,256,1]{2,1,0:T(8,128)S(1)} %get-tuple-element.87), channel_id=1, source_target_pairs={{0,16},{16,32},{32,48},{48,64},{64,80},{80,96},{96,112},{1,17},{17... | collective-permute-start | bytes 6152 | tf_op jit(solution)/shard_map/ppermute | solution.py:25
  375.4 8.5 %collective-permute-start.62 = (f32[2,1,258]{2,1,0:T(1,128)S(1)}, f32[2,1,258]{2,1,0:T(1,128)S(1)}, u32[]{:S(2)}, u32[]{:S(2)}) collective-permute-start(f32[2,1,258]{2,1,0:T(1,128)S(1)} %get-tuple-element.36), channel_id=1, source_target_pairs={{0,1},{1,2},{2,3},{3,4},{4,5},{5,6},{6,7},{7,8},{8,9},{9,10},{10,1... | collective-permute-start | bytes 6200 | tf_op jit(solution)/shard_map/ppermute | solution.py:25
  388.3 7.1 %collective-permute-start.64 = (f32[2,256,1]{2,1,0:T(8,128)S(1)}, f32[2,256,1]{2,1,0:T(8,128)S(1)}, u32[]{:S(2)}, u32[]{:S(2)}) collective-permute-start(f32[2,256,1]{2,1,0:T(8,128)S(1)} %get-tuple-element.85), channel_id=1, source_target_pairs={{0,16},{16,32},{32,48},{48,64},{64,80},{80,96},{96,112},{1,17},{17... | collective-permute-start | bytes 6152 | tf_op jit(solution)/shard_map/ppermute | solution.py:25
  399.4 7.7 %collective-permute-start.66 = (f32[2,1,258]{2,1,0:T(1,128)S(1)}, f32[2,1,258]{2,1,0:T(1,128)S(1)}, u32[]{:S(2)}, u32[]{:S(2)}) collective-permute-start(f32[2,1,258]{2,1,0:T(1,128)S(1)} %get-tuple-element.34), channel_id=1, source_target_pairs={{0,1},{1,2},{2,3},{3,4},{4,5},{5,6},{6,7},{7,8},{8,9},{9,10},{10,1... | collective-permute-start | bytes 6200 | tf_op jit(solution)/shard_map/ppermute | solution.py:25
  409.0 7.8 %collective-permute-done.67 = f32[2,1,258]{2,1,0:T(1,128)S(1)} collective-permute-done((f32[2,1,258]{2,1,0:T(1,128)S(1)}, f32[2,1,258]{2,1,0:T(1,128)S(1)}, u32[]{:S(2)}, u32[]{:S(2)}) %collective-permute-start.67) | collective-permute-done | bytes 2096 | tf_op jit(solution)/shard_map/ppermute | solution.py:27
  419.0 10.1 %reshape.213 = f32[64,4,64,4]{3,2,1,0:T(8,128)} reshape(f32[256,256]{1,0:T(8,128)S(1)} %fusion.161) | data formatting | bytes 524288 | tf_op jit(solution)/shard_map/reshape | solution.py:126
  435.7 188.1 %all-reduce.6.cloned.1.call-done = f32[64,4096]{1,0:T(8,128)} async-done(((f32[64,4096]{1,0:T(8,128)}), f32[64,4096]{1,0:T(8,128)}) %all-reduce.6.cloned.1.call-update) | async-done | bytes 1048592
  625.4 75.7 %all-reduce.4.cloned.1.call-done = f32[4,4096]{1,0:T(4,128)} async-done(((f32[4,4096]{1,0:T(4,128)}), f32[4,4096]{1,0:T(4,128)}) %all-reduce.4.cloned.1.call-update) | async-done | bytes 65552 | tf_op jit(solution)/shard_map/psum | solution.py:136
  (296 shorter events, 223.0 us)
Async XLA Ops:
  7.2 57.2 %all-gather.3.cloned.1.call-start = ((), (), s32[]{:S(2)}) async-start(), calls=%async_computation.1 | async-start | bytes 1114112 | tf_op jit(solution)/shard_map/all_gather | solution.py:100
  7.3 10.2 %collective-permute-start.1 = (f32[2,256,1]{2,1,0:T(8,128)S(1)}, f32[2,256,1]{2,1,0:T(8,128)S(1)}, u32[]{:S(2)}, u32[]{:S(2)}) collective-permute-start(f32[2,256,1]{2,1,0:T(8,128)S(1)} %broadcast.112), channel_id=1, source_target_pairs={{16,0},{32,16},{48,32},{64,48},{80,64},{96,80},{112,96},{17,1},{33... | collective-permute-start | bytes 6152 | tf_op jit(solution)/shard_map/ppermute | solution.py:27
  8.6 10.1 %collective-permute-start = (f32[2,256,1]{2,1,0:T(8,128)S(1)}, f32[2,256,1]{2,1,0:T(8,128)S(1)}, u32[]{:S(2)}, u32[]{:S(2)}) collective-permute-start(f32[2,256,1]{2,1,0:T(8,128)S(1)} %broadcast.112), channel_id=1, source_target_pairs={{0,16},{16,32},{32,48},{48,64},{64,80},{80,96},{96,112},{1,17},{17... | collective-permute-start | bytes 6152 | tf_op jit(solution)/shard_map/ppermute | solution.py:25
  14.6 609.2 %all-reduce.6.cloned.1.call-start = ((), (), s32[]{:S(2)}) async-start(), calls=%async_computation.2 | async-start | bytes 2097152
  89.2 10.4 %collective-permute-start.9 = (f32[2,256,1]{2,1,0:T(8,128)S(1)}, f32[2,256,1]{2,1,0:T(8,128)S(1)}, u32[]{:S(2)}, u32[]{:S(2)}) collective-permute-start(f32[2,256,1]{2,1,0:T(8,128)S(1)} %get-tuple-element.108), channel_id=1, source_target_pairs={{16,0},{32,16},{48,32},{64,48},{80,64},{96,80},{112,96},{17,1},{33... | collective-permute-start | bytes 6152 | tf_op jit(solution)/shard_map/ppermute | solution.py:27
  90.5 10.4 %collective-permute-start.8 = (f32[2,256,1]{2,1,0:T(8,128)S(1)}, f32[2,256,1]{2,1,0:T(8,128)S(1)}, u32[]{:S(2)}, u32[]{:S(2)}) collective-permute-start(f32[2,256,1]{2,1,0:T(8,128)S(1)} %get-tuple-element.107), channel_id=1, source_target_pairs={{0,16},{16,32},{32,48},{48,64},{64,80},{80,96},{96,112},{1,17},{17... | collective-permute-start | bytes 6152 | tf_op jit(solution)/shard_map/ppermute | solution.py:25
  108.8 11.4 %collective-permute-start.13 = (f32[2,256,1]{2,1,0:T(8,128)S(1)}, f32[2,256,1]{2,1,0:T(8,128)S(1)}, u32[]{:S(2)}, u32[]{:S(2)}) collective-permute-start(f32[2,256,1]{2,1,0:T(8,128)S(1)} %get-tuple-element.106), channel_id=1, source_target_pairs={{16,0},{32,16},{48,32},{64,48},{80,64},{96,80},{112,96},{17,1},{33... | collective-permute-start | bytes 6152 | tf_op jit(solution)/shard_map/ppermute | solution.py:27
  110.1 11.7 %collective-permute-start.12 = (f32[2,256,1]{2,1,0:T(8,128)S(1)}, f32[2,256,1]{2,1,0:T(8,128)S(1)}, u32[]{:S(2)}, u32[]{:S(2)}) collective-permute-start(f32[2,256,1]{2,1,0:T(8,128)S(1)} %get-tuple-element.105), channel_id=1, source_target_pairs={{0,16},{16,32},{32,48},{48,64},{64,80},{80,96},{96,112},{1,17},{17... | collective-permute-start | bytes 6152 | tf_op jit(solution)/shard_map/ppermute | solution.py:25
  145.6 10.7 %collective-permute-start.21 = (f32[2,256,1]{2,1,0:T(8,128)S(1)}, f32[2,256,1]{2,1,0:T(8,128)S(1)}, u32[]{:S(2)}, u32[]{:S(2)}) collective-permute-start(f32[2,256,1]{2,1,0:T(8,128)S(1)} %get-tuple-element.104), channel_id=1, source_target_pairs={{16,0},{32,16},{48,32},{64,48},{80,64},{96,80},{112,96},{17,1},{33... | collective-permute-start | bytes 6152 | tf_op jit(solution)/shard_map/ppermute | solution.py:27
  146.9 11.2 %collective-permute-start.20 = (f32[2,256,1]{2,1,0:T(8,128)S(1)}, f32[2,256,1]{2,1,0:T(8,128)S(1)}, u32[]{:S(2)}, u32[]{:S(2)}) collective-permute-start(f32[2,256,1]{2,1,0:T(8,128)S(1)} %get-tuple-element.103), channel_id=1, source_target_pairs={{0,16},{16,32},{32,48},{48,64},{64,80},{80,96},{96,112},{1,17},{17... | collective-permute-start | bytes 6152 | tf_op jit(solution)/shard_map/ppermute | solution.py:25
  166.1 11.6 %collective-permute-start.25 = (f32[2,256,1]{2,1,0:T(8,128)S(1)}, f32[2,256,1]{2,1,0:T(8,128)S(1)}, u32[]{:S(2)}, u32[]{:S(2)}) collective-permute-start(f32[2,256,1]{2,1,0:T(8,128)S(1)} %get-tuple-element.102), channel_id=1, source_target_pairs={{16,0},{32,16},{48,32},{64,48},{80,64},{96,80},{112,96},{17,1},{33... | collective-permute-start | bytes 6152 | tf_op jit(solution)/shard_map/ppermute | solution.py:27
  167.4 12.1 %collective-permute-start.24 = (f32[2,256,1]{2,1,0:T(8,128)S(1)}, f32[2,256,1]{2,1,0:T(8,128)S(1)}, u32[]{:S(2)}, u32[]{:S(2)}) collective-permute-start(f32[2,256,1]{2,1,0:T(8,128)S(1)} %get-tuple-element.101), channel_id=1, source_target_pairs={{0,16},{16,32},{32,48},{48,64},{64,80},{80,96},{96,112},{1,17},{17... | collective-permute-start | bytes 6152 | tf_op jit(solution)/shard_map/ppermute | solution.py:25
  187.6 9.6 %collective-permute-start.29 = (f32[256,1]{1,0:T(8,128)S(1)}, f32[256,1]{1,0:T(8,128)S(1)}, u32[]{:S(2)}, u32[]{:S(2)}) collective-permute-start(f32[256,1]{1,0:T(8,128)S(1)} %get-tuple-element.142), channel_id=1, source_target_pairs={{0,16},{16,32},{32,48},{48,64},{64,80},{80,96},{96,112},{1,17},{17... | collective-permute-start | bytes 3080 | tf_op jit(solution)/shard_map/ppermute | solution.py:25
  205.6 11.2 %collective-permute-start.33 = (f32[2,256,1]{2,1,0:T(8,128)S(1)}, f32[2,256,1]{2,1,0:T(8,128)S(1)}, u32[]{:S(2)}, u32[]{:S(2)}) collective-permute-start(f32[2,256,1]{2,1,0:T(8,128)S(1)} %get-tuple-element.100), channel_id=1, source_target_pairs={{16,0},{32,16},{48,32},{64,48},{80,64},{96,80},{112,96},{17,1},{33... | collective-permute-start | bytes 6152 | tf_op jit(solution)/shard_map/ppermute | solution.py:27
  206.9 11.6 %collective-permute-start.32 = (f32[2,256,1]{2,1,0:T(8,128)S(1)}, f32[2,256,1]{2,1,0:T(8,128)S(1)}, u32[]{:S(2)}, u32[]{:S(2)}) collective-permute-start(f32[2,256,1]{2,1,0:T(8,128)S(1)} %get-tuple-element.99), channel_id=1, source_target_pairs={{0,16},{16,32},{32,48},{48,64},{64,80},{80,96},{96,112},{1,17},{17... | collective-permute-start | bytes 6152 | tf_op jit(solution)/shard_map/ppermute | solution.py:25
  228.2 10.8 %collective-permute-start.37 = (f32[2,256,1]{2,1,0:T(8,128)S(1)}, f32[2,256,1]{2,1,0:T(8,128)S(1)}, u32[]{:S(2)}, u32[]{:S(2)}) collective-permute-start(f32[2,256,1]{2,1,0:T(8,128)S(1)} %get-tuple-element.98), channel_id=1, source_target_pairs={{16,0},{32,16},{48,32},{64,48},{80,64},{96,80},{112,96},{17,1},{33... | collective-permute-start | bytes 6152 | tf_op jit(solution)/shard_map/ppermute | solution.py:27
  229.5 11.0 %collective-permute-start.36 = (f32[2,256,1]{2,1,0:T(8,128)S(1)}, f32[2,256,1]{2,1,0:T(8,128)S(1)}, u32[]{:S(2)}, u32[]{:S(2)}) collective-permute-start(f32[2,256,1]{2,1,0:T(8,128)S(1)} %get-tuple-element.97), channel_id=1, source_target_pairs={{0,16},{16,32},{32,48},{48,64},{64,80},{80,96},{96,112},{1,17},{17... | collective-permute-start | bytes 6152 | tf_op jit(solution)/shard_map/ppermute | solution.py:25
  269.7 11.2 %collective-permute-start.45 = (f32[2,256,1]{2,1,0:T(8,128)S(1)}, f32[2,256,1]{2,1,0:T(8,128)S(1)}, u32[]{:S(2)}, u32[]{:S(2)}) collective-permute-start(f32[2,256,1]{2,1,0:T(8,128)S(1)} %get-tuple-element.96), channel_id=1, source_target_pairs={{16,0},{32,16},{48,32},{64,48},{80,64},{96,80},{112,96},{17,1},{33... | collective-permute-start | bytes 6152 | tf_op jit(solution)/shard_map/ppermute | solution.py:27
  271.0 11.7 %collective-permute-start.44 = (f32[2,256,1]{2,1,0:T(8,128)S(1)}, f32[2,256,1]{2,1,0:T(8,128)S(1)}, u32[]{:S(2)}, u32[]{:S(2)}) collective-permute-start(f32[2,256,1]{2,1,0:T(8,128)S(1)} %get-tuple-element.95), channel_id=1, source_target_pairs={{0,16},{16,32},{32,48},{48,64},{64,80},{80,96},{96,112},{1,17},{17... | collective-permute-start | bytes 6152 | tf_op jit(solution)/shard_map/ppermute | solution.py:25
  294.1 11.3 %collective-permute-start.49 = (f32[2,256,1]{2,1,0:T(8,128)S(1)}, f32[2,256,1]{2,1,0:T(8,128)S(1)}, u32[]{:S(2)}, u32[]{:S(2)}) collective-permute-start(f32[2,256,1]{2,1,0:T(8,128)S(1)} %get-tuple-element.94), channel_id=1, source_target_pairs={{16,0},{32,16},{48,32},{64,48},{80,64},{96,80},{112,96},{17,1},{33... | collective-permute-start | bytes 6152 | tf_op jit(solution)/shard_map/ppermute | solution.py:27
  295.4 11.7 %collective-permute-start.48 = (f32[2,256,1]{2,1,0:T(8,128)S(1)}, f32[2,256,1]{2,1,0:T(8,128)S(1)}, u32[]{:S(2)}, u32[]{:S(2)}) collective-permute-start(f32[2,256,1]{2,1,0:T(8,128)S(1)} %get-tuple-element.93), channel_id=1, source_target_pairs={{0,16},{16,32},{32,48},{48,64},{64,80},{80,96},{96,112},{1,17},{17... | collective-permute-start | bytes 6152 | tf_op jit(solution)/shard_map/ppermute | solution.py:25
  316.6 11.7 %collective-permute-start.53 = (f32[2,256,1]{2,1,0:T(8,128)S(1)}, f32[2,256,1]{2,1,0:T(8,128)S(1)}, u32[]{:S(2)}, u32[]{:S(2)}) collective-permute-start(f32[2,256,1]{2,1,0:T(8,128)S(1)} %get-tuple-element.92), channel_id=1, source_target_pairs={{16,0},{32,16},{48,32},{64,48},{80,64},{96,80},{112,96},{17,1},{33... | collective-permute-start | bytes 6152 | tf_op jit(solution)/shard_map/ppermute | solution.py:27
  317.9 12.1 %collective-permute-start.52 = (f32[2,256,1]{2,1,0:T(8,128)S(1)}, f32[2,256,1]{2,1,0:T(8,128)S(1)}, u32[]{:S(2)}, u32[]{:S(2)}) collective-permute-start(f32[2,256,1]{2,1,0:T(8,128)S(1)} %get-tuple-element.91), channel_id=1, source_target_pairs={{0,16},{16,32},{32,48},{48,64},{64,80},{80,96},{96,112},{1,17},{17... | collective-permute-start | bytes 6152 | tf_op jit(solution)/shard_map/ppermute | solution.py:25
  339.0 10.5 %collective-permute-start.57 = (f32[2,256,1]{2,1,0:T(8,128)S(1)}, f32[2,256,1]{2,1,0:T(8,128)S(1)}, u32[]{:S(2)}, u32[]{:S(2)}) collective-permute-start(f32[2,256,1]{2,1,0:T(8,128)S(1)} %get-tuple-element.90), channel_id=1, source_target_pairs={{16,0},{32,16},{48,32},{64,48},{80,64},{96,80},{112,96},{17,1},{33... | collective-permute-start | bytes 6152 | tf_op jit(solution)/shard_map/ppermute | solution.py:27
  340.3 10.7 %collective-permute-start.56 = (f32[2,256,1]{2,1,0:T(8,128)S(1)}, f32[2,256,1]{2,1,0:T(8,128)S(1)}, u32[]{:S(2)}, u32[]{:S(2)}) collective-permute-start(f32[2,256,1]{2,1,0:T(8,128)S(1)} %get-tuple-element.89), channel_id=1, source_target_pairs={{0,16},{16,32},{32,48},{48,64},{64,80},{80,96},{96,112},{1,17},{17... | collective-permute-start | bytes 6152 | tf_op jit(solution)/shard_map/ppermute | solution.py:25
  361.7 10.8 %collective-permute-start.61 = (f32[2,256,1]{2,1,0:T(8,128)S(1)}, f32[2,256,1]{2,1,0:T(8,128)S(1)}, u32[]{:S(2)}, u32[]{:S(2)}) collective-permute-start(f32[2,256,1]{2,1,0:T(8,128)S(1)} %get-tuple-element.88), channel_id=1, source_target_pairs={{16,0},{32,16},{48,32},{64,48},{80,64},{96,80},{112,96},{17,1},{33... | collective-permute-start | bytes 6152 | tf_op jit(solution)/shard_map/ppermute | solution.py:27
  363.0 11.0 %collective-permute-start.60 = (f32[2,256,1]{2,1,0:T(8,128)S(1)}, f32[2,256,1]{2,1,0:T(8,128)S(1)}, u32[]{:S(2)}, u32[]{:S(2)}) collective-permute-start(f32[2,256,1]{2,1,0:T(8,128)S(1)} %get-tuple-element.87), channel_id=1, source_target_pairs={{0,16},{16,32},{32,48},{48,64},{64,80},{80,96},{96,112},{1,17},{17... | collective-permute-start | bytes 6152 | tf_op jit(solution)/shard_map/ppermute | solution.py:25
  374.1 9.8 %collective-permute-start.63 = (f32[2,1,258]{2,1,0:T(1,128)S(1)}, f32[2,1,258]{2,1,0:T(1,128)S(1)}, u32[]{:S(2)}, u32[]{:S(2)}) collective-permute-start(f32[2,1,258]{2,1,0:T(1,128)S(1)} %get-tuple-element.35), channel_id=1, source_target_pairs={{1,0},{2,1},{3,2},{4,3},{5,4},{6,5},{7,6},{8,7},{9,8},{10,9},{11,1... | collective-permute-start | bytes 6200 | tf_op jit(solution)/shard_map/ppermute | solution.py:27
  387.0 10.8 %collective-permute-start.65 = (f32[2,256,1]{2,1,0:T(8,128)S(1)}, f32[2,256,1]{2,1,0:T(8,128)S(1)}, u32[]{:S(2)}, u32[]{:S(2)}) collective-permute-start(f32[2,256,1]{2,1,0:T(8,128)S(1)} %get-tuple-element.86), channel_id=1, source_target_pairs={{16,0},{32,16},{48,32},{64,48},{80,64},{96,80},{112,96},{17,1},{33... | collective-permute-start | bytes 6152 | tf_op jit(solution)/shard_map/ppermute | solution.py:27
  388.3 11.0 %collective-permute-start.64 = (f32[2,256,1]{2,1,0:T(8,128)S(1)}, f32[2,256,1]{2,1,0:T(8,128)S(1)}, u32[]{:S(2)}, u32[]{:S(2)}) collective-permute-start(f32[2,256,1]{2,1,0:T(8,128)S(1)} %get-tuple-element.85), channel_id=1, source_target_pairs={{0,16},{16,32},{32,48},{48,64},{64,80},{80,96},{96,112},{1,17},{17... | collective-permute-start | bytes 6152 | tf_op jit(solution)/shard_map/ppermute | solution.py:25
  407.1 9.7 %collective-permute-start.67 = (f32[2,1,258]{2,1,0:T(1,128)S(1)}, f32[2,1,258]{2,1,0:T(1,128)S(1)}, u32[]{:S(2)}, u32[]{:S(2)}) collective-permute-start(f32[2,1,258]{2,1,0:T(1,128)S(1)} %get-tuple-element.33), channel_id=1, source_target_pairs={{1,0},{2,1},{3,2},{4,3},{5,4},{6,5},{7,6},{8,7},{9,8},{10,9},{11,1... | collective-permute-start | bytes 6200 | tf_op jit(solution)/shard_map/ppermute | solution.py:27
  434.4 266.7 %all-reduce.4.cloned.1.call-start = ((), (), s32[]{:S(2)}) async-start(), calls=%async_computation | async-start | bytes 131072 | tf_op jit(solution)/shard_map/psum | solution.py:136
  (54 other events, 853.7 us)
Sparse Core Ops, SparseCore 0:
  14.8 49.5 all-gather.2
  434.5 189.2 all-reduce.5
  627.0 74.0 all-reduce.3
where the time goes:
time: 719 us; the launch traced here: 709 us
  waiting for transfers between devices  373 us (52%)
  starting transfers between devices  229 us (32%)
  other arithmetic  48.5 us (7%)
  local copies, waits for them, and re-layouts  37.6 us (5%)
  between operations  16.9 us (2%)
    unnamed x4, waiting for transfers between devices  188 us
    ppermute x34, starting transfers between devices, with_halo(): lax.ppermute(tail, axis, [(i, (i + 1) % count) for i in range(ends)])  185 us
    psum x1, waiting for transfers between devices, per_device(): gradient = lax.psum(partial_sum, 'gx')  75.7 us
    ppermute x34, waiting for transfers between devices, with_halo(): lax.ppermute(head, axis, [((i + 1) % count, i) for i in range(ends)])  53.8 us
    ppermute x34, starting transfers between devices, with_halo(): lax.ppermute(head, axis, [((i + 1) % count, i) for i in range(ends)])  43.9 us
    ppermute x34, waiting for transfers between devices, with_halo(): lax.ppermute(tail, axis, [(i, (i + 1) % count) for i in range(ends)])  35.8 us
    all_gather x1, waiting for transfers between devices, per_device(): shard_rows = lax.all_gather(rates, 'gy', axis=0, tiled=True)  19.9 us
    another operation x36, other arithmetic, relaxation(): return jnp.stack([new_u, new_v])  15.8 us
  transfers between devices with their start and end apart: 71, of which 52 were waited for; matrix products, arithmetic and copies ran while one was open for 2% of the time, Pallas kernels for 0%

commit v1 on v0

--- a/solution.py
+++ b/solution.py
@@ -12,6 +12,11 @@
 COARSE = 4096
 visc_scale = 0.1
 strain_floor = 0.05
+
+
+def add_all(shard, axis):
+    blocks = lax.all_gather(shard, axis)
+    return jnp.sum(blocks, axis=0)
 
 
 def with_halo(cells, sides, width):
@@ -133,7 +138,7 @@
         scatter_dimension=0,
         tiled=True,
     )
-    gradient = lax.psum(partial_sum, "gx")
+    gradient = add_all(partial_sum, "gx")
     return (velocity[0], velocity[1], gradient)
 
 

time: 719 us -> 671 us (0.933)
  waiting for transfers between devices: 373 us -> 299 us
  blocking collectives: 0 us -> 29 us
    psum x1 -> x0, waiting for transfers between devices: 75.7 us -> none  [per_device(): gradient = lax.psum(partial_sum, 'gx')]
    all_gather x0 -> x1, blocking collectives: none -> 29 us  [add_all(): blocks = lax.all_gather(shard, axis)]
    unnamed x4 -> x3, waiting for transfers between devices: 188 us -> 188 us
  transfers between devices with their start and end apart: 71 -> 70, of which waited for: 52 -> 51; matrix products, arithmetic and copies ran while one was open for 2% -> 2% of each run, Pallas kernels for 0% -> 0%
where the time goes in v1:
time: 671 us; the launch traced here: 661 us
  waiting for transfers between devices  299 us (45%)
  starting transfers between devices  229 us (34%)
  other arithmetic  49.1 us (7%)
  local copies, waits for them, and re-layouts  34.7 us (5%)
  blocking collectives  29 us (4%)
  between operations  17.2 us (3%)
    unnamed x3, waiting for transfers between devices  188 us
    ppermute x34, starting transfers between devices, with_halo(): lax.ppermute(tail, axis, [(i, (i + 1) % count) for i in range(ends)])  185 us
    ppermute x34, waiting for transfers between devices, with_halo(): lax.ppermute(head, axis, [((i + 1) % count, i) for i in range(ends)])  53.8 us
    ppermute x34, starting transfers between devices, with_halo(): lax.ppermute(head, axis, [((i + 1) % count, i) for i in range(ends)])  43.9 us
    ppermute x34, waiting for transfers between devices, with_halo(): lax.ppermute(tail, axis, [(i, (i + 1) % count) for i in range(ends)])  35.9 us
    all_gather x1, blocking collectives, add_all(): blocks = lax.all_gather(shard, axis)  29 us
    all_gather x1, waiting for transfers between devices, per_device(): shard_rows = lax.all_gather(rates, 'gy', axis=0, tiled=True)  20.7 us
    another operation x36, other arithmetic, relaxation(): return jnp.stack([new_u, new_v])  15.8 us
  transfers between devices with their start and end apart: 70, of which 51 were waited for; matrix products, arithmetic and copies ran while one was open for 2% of the time, Pallas kernels for 0%

profile of v1, /device:TPU:0, one launch (start us, length us, event | category | flops | bytes accessed | tf_op | source)
XLA Modules:
  0.0 661.4 jit_solution(17884321620362670657)
XLA Ops:
  8.6 4.6 collective-permute-start
  26.5 5.0 collective-permute-start.5
  43.7 20.7 %all-gather.5.cloned.1.call-done = f32[16,4,4096]{2,1,0:T(4,128)} async-done(((f32[1,4,4096]{2,1,0:T(4,128)}), f32[16,4,4096]{2,1,0:T(4,128)}) %all-gather.5.cloned.1.call-update) | async-done | bytes 1048592 | tf_op jit(solution)/shard_map/all_gather | solution.py:105
  78.0 8.4 %broadcast_in_dim.8 = f32[256,256]{1,0:T(8,128)S(1)} reshape(f32[64,4,64,4]{3,2,1,0:T(8,128)} %broadcast_in_dim.7) | data formatting | bytes 524288 | tf_op jit(solution)/shard_map/broadcast_in_dim | solution.py:109
  90.5 4.7 collective-permute-start.8
  110.0 5.2 collective-permute-start.12
  115.2 5.0 collective-permute-done.13
  129.5 5.0 collective-permute-start.17
  146.8 5.0 collective-permute-start.20
  167.3 6.2 collective-permute-start.24
  187.5 7.1 %collective-permute-start.29 = (f32[256,1]{1,0:T(8,128)S(1)}, f32[256,1]{1,0:T(8,128)S(1)}, u32[]{:S(2)}, u32[]{:S(2)}) collective-permute-start(f32[256,1]{1,0:T(8,128)S(1)} %get-tuple-element.142), channel_id=1, source_target_pairs={{0,16},{16,32},{32,48},{48,64},{64,80},{80,96},{96,112},{1,17},{17... | collective-permute-start | bytes 3080 | tf_op jit(solution)/shard_map/ppermute | solution.py:30
  206.9 7.1 %collective-permute-start.32 = (f32[2,256,1]{2,1,0:T(8,128)S(1)}, f32[2,256,1]{2,1,0:T(8,128)S(1)}, u32[]{:S(2)}, u32[]{:S(2)}) collective-permute-start(f32[2,256,1]{2,1,0:T(8,128)S(1)} %get-tuple-element.99), channel_id=1, source_target_pairs={{0,16},{16,32},{32,48},{48,64},{64,80},{80,96},{96,112},{1,17},{17... | collective-permute-start | bytes 6152 | tf_op jit(solution)/shard_map/ppermute | solution.py:30
  219.9 4.8 collective-permute-start.34
  229.4 7.1 %collective-permute-start.36 = (f32[2,256,1]{2,1,0:T(8,128)S(1)}, f32[2,256,1]{2,1,0:T(8,128)S(1)}, u32[]{:S(2)}, u32[]{:S(2)}) collective-permute-start(f32[2,256,1]{2,1,0:T(8,128)S(1)} %get-tuple-element.97), channel_id=1, source_target_pairs={{0,16},{16,32},{32,48},{48,64},{64,80},{80,96},{96,112},{1,17},{17... | collective-permute-start | bytes 6152 | tf_op jit(solution)/shard_map/ppermute | solution.py:30
  241.8 5.5 collective-permute-start.38
  250.6 7.1 %collective-permute-start.41 = (f32[256,1]{1,0:T(8,128)S(1)}, f32[256,1]{1,0:T(8,128)S(1)}, u32[]{:S(2)}, u32[]{:S(2)}) collective-permute-start(f32[256,1]{1,0:T(8,128)S(1)} %get-tuple-element.140), channel_id=1, source_target_pairs={{0,16},{16,32},{32,48},{48,64},{64,80},{80,96},{96,112},{1,17},{17... | collective-permute-start | bytes 3080 | tf_op jit(solution)/shard_map/ppermute | solution.py:30
  262.0 5.2 collective-permute-start.43
  271.0 7.1 %collective-permute-start.44 = (f32[2,256,1]{2,1,0:T(8,128)S(1)}, f32[2,256,1]{2,1,0:T(8,128)S(1)}, u32[]{:S(2)}, u32[]{:S(2)}) collective-permute-start(f32[2,256,1]{2,1,0:T(8,128)S(1)} %get-tuple-element.95), channel_id=1, source_target_pairs={{0,16},{16,32},{32,48},{48,64},{64,80},{80,96},{96,112},{1,17},{17... | collective-permute-start | bytes 6152 | tf_op jit(solution)/shard_map/ppermute | solution.py:30
  284.0 5.2 collective-permute-start.46
  295.4 7.1 %collective-permute-start.48 = (f32[2,256,1]{2,1,0:T(8,128)S(1)}, f32[2,256,1]{2,1,0:T(8,128)S(1)}, u32[]{:S(2)}, u32[]{:S(2)}) collective-permute-start(f32[2,256,1]{2,1,0:T(8,128)S(1)} %get-tuple-element.93), channel_id=1, source_target_pairs={{0,16},{16,32},{32,48},{48,64},{64,80},{80,96},{96,112},{1,17},{17... | collective-permute-start | bytes 6152 | tf_op jit(solution)/shard_map/ppermute | solution.py:30
  308.5 4.8 collective-permute-start.50
  317.8 7.1 %collective-permute-start.52 = (f32[2,256,1]{2,1,0:T(8,128)S(1)}, f32[2,256,1]{2,1,0:T(8,128)S(1)}, u32[]{:S(2)}, u32[]{:S(2)}) collective-permute-start(f32[2,256,1]{2,1,0:T(8,128)S(1)} %get-tuple-element.91), channel_id=1, source_target_pairs={{0,16},{16,32},{32,48},{48,64},{64,80},{80,96},{96,112},{1,17},{17... | collective-permute-start | bytes 6152 | tf_op jit(solution)/shard_map/ppermute | solution.py:30
  340.2 6.8 %collective-permute-start.56 = (f32[2,256,1]{2,1,0:T(8,128)S(1)}, f32[2,256,1]{2,1,0:T(8,128)S(1)}, u32[]{:S(2)}, u32[]{:S(2)}) collective-permute-start(f32[2,256,1]{2,1,0:T(8,128)S(1)} %get-tuple-element.89), channel_id=1, source_target_pairs={{0,16},{16,32},{32,48},{48,64},{64,80},{80,96},{96,112},{1,17},{17... | collective-permute-start | bytes 6152 | tf_op jit(solution)/shard_map/ppermute | solution.py:30
  352.3 6.1 collective-permute-start.58
  363.0 7.1 %collective-permute-start.60 = (f32[2,256,1]{2,1,0:T(8,128)S(1)}, f32[2,256,1]{2,1,0:T(8,128)S(1)}, u32[]{:S(2)}, u32[]{:S(2)}) collective-permute-start(f32[2,256,1]{2,1,0:T(8,128)S(1)} %get-tuple-element.87), channel_id=1, source_target_pairs={{0,16},{16,32},{32,48},{48,64},{64,80},{80,96},{96,112},{1,17},{17... | collective-permute-start | bytes 6152 | tf_op jit(solution)/shard_map/ppermute | solution.py:30
  375.4 8.5 %collective-permute-start.62 = (f32[2,1,258]{2,1,0:T(1,128)S(1)}, f32[2,1,258]{2,1,0:T(1,128)S(1)}, u32[]{:S(2)}, u32[]{:S(2)}) collective-permute-start(f32[2,1,258]{2,1,0:T(1,128)S(1)} %get-tuple-element.36), channel_id=1, source_target_pairs={{0,1},{1,2},{2,3},{3,4},{4,5},{5,6},{6,7},{7,8},{8,9},{9,10},{10,1... | collective-permute-start | bytes 6200 | tf_op jit(solution)/shard_map/ppermute | solution.py:30
  388.3 7.1 %collective-permute-start.64 = (f32[2,256,1]{2,1,0:T(8,128)S(1)}, f32[2,256,1]{2,1,0:T(8,128)S(1)}, u32[]{:S(2)}, u32[]{:S(2)}) collective-permute-start(f32[2,256,1]{2,1,0:T(8,128)S(1)} %get-tuple-element.85), channel_id=1, source_target_pairs={{0,16},{16,32},{32,48},{48,64},{64,80},{80,96},{96,112},{1,17},{17... | collective-permute-start | bytes 6152 | tf_op jit(solution)/shard_map/ppermute | solution.py:30
  399.4 7.7 %collective-permute-start.66 = (f32[2,1,258]{2,1,0:T(1,128)S(1)}, f32[2,1,258]{2,1,0:T(1,128)S(1)}, u32[]{:S(2)}, u32[]{:S(2)}) collective-permute-start(f32[2,1,258]{2,1,0:T(1,128)S(1)} %get-tuple-element.34), channel_id=1, source_target_pairs={{0,1},{1,2},{2,3},{3,4},{4,5},{5,6},{6,7},{7,8},{8,9},{9,10},{10,1... | collective-permute-start | bytes 6200 | tf_op jit(solution)/shard_map/ppermute | solution.py:30
  409.0 7.8 %collective-permute-done.67 = f32[2,1,258]{2,1,0:T(1,128)S(1)} collective-permute-done((f32[2,1,258]{2,1,0:T(1,128)S(1)}, f32[2,1,258]{2,1,0:T(1,128)S(1)}, u32[]{:S(2)}, u32[]{:S(2)}) %collective-permute-start.67) | collective-permute-done | bytes 2096 | tf_op jit(solution)/shard_map/ppermute | solution.py:32
  419.0 10.1 %reshape.213 = f32[64,4,64,4]{3,2,1,0:T(8,128)} reshape(f32[256,256]{1,0:T(8,128)S(1)} %fusion.161) | data formatting | bytes 524288 | tf_op jit(solution)/shard_map/reshape | solution.py:131
  435.6 188.2 %all-reduce.3.cloned.1.call-done = f32[64,4096]{1,0:T(8,128)} async-done(((f32[64,4096]{1,0:T(8,128)}), f32[64,4096]{1,0:T(8,128)}) %all-reduce.3.cloned.1.call-update) | async-done | bytes 1048592
  624.7 29.0 %all-gather.2 = f32[8,4,4096]{2,1,0:T(4,128)S(1)} all-gather(f32[1,4,4096]{2,1,0:T(4,128)S(1)} %dynamic-slice_bitcast_fusion), channel_id=2, replica_groups=mesh['gx'=8,'gy'=16] {'gx'}, dimensions={0}, use_global_device_ids=true | all-gather | bytes 589824 | tf_op jit(solution)/shard_map/all_gather | solution.py:18
  (294 shorter events, 220.8 us)
Async XLA Ops:
  7.2 57.2 %all-gather.5.cloned.1.call-start = ((), (), s32[]{:S(2)}) async-start(), calls=%async_computation | async-start | bytes 1114112 | tf_op jit(solution)/shard_map/all_gather | solution.py:105
  7.3 10.2 %collective-permute-start.1 = (f32[2,256,1]{2,1,0:T(8,128)S(1)}, f32[2,256,1]{2,1,0:T(8,128)S(1)}, u32[]{:S(2)}, u32[]{:S(2)}) collective-permute-start(f32[2,256,1]{2,1,0:T(8,128)S(1)} %broadcast.112), channel_id=1, source_target_pairs={{16,0},{32,16},{48,32},{64,48},{80,64},{96,80},{112,96},{17,1},{33... | collective-permute-start | bytes 6152 | tf_op jit(solution)/shard_map/ppermute | solution.py:32
  8.6 10.1 %collective-permute-start = (f32[2,256,1]{2,1,0:T(8,128)S(1)}, f32[2,256,1]{2,1,0:T(8,128)S(1)}, u32[]{:S(2)}, u32[]{:S(2)}) collective-permute-start(f32[2,256,1]{2,1,0:T(8,128)S(1)} %broadcast.112), channel_id=1, source_target_pairs={{0,16},{16,32},{32,48},{48,64},{64,80},{80,96},{96,112},{1,17},{17... | collective-permute-start | bytes 6152 | tf_op jit(solution)/shard_map/ppermute | solution.py:30
  14.6 609.1 %all-reduce.3.cloned.1.call-start = ((), (), s32[]{:S(2)}) async-start(), calls=%async_computation.1 | async-start | bytes 2097152
  89.2 10.4 %collective-permute-start.9 = (f32[2,256,1]{2,1,0:T(8,128)S(1)}, f32[2,256,1]{2,1,0:T(8,128)S(1)}, u32[]{:S(2)}, u32[]{:S(2)}) collective-permute-start(f32[2,256,1]{2,1,0:T(8,128)S(1)} %get-tuple-element.108), channel_id=1, source_target_pairs={{16,0},{32,16},{48,32},{64,48},{80,64},{96,80},{112,96},{17,1},{33... | collective-permute-start | bytes 6152 | tf_op jit(solution)/shard_map/ppermute | solution.py:32
  90.5 10.4 %collective-permute-start.8 = (f32[2,256,1]{2,1,0:T(8,128)S(1)}, f32[2,256,1]{2,1,0:T(8,128)S(1)}, u32[]{:S(2)}, u32[]{:S(2)}) collective-permute-start(f32[2,256,1]{2,1,0:T(8,128)S(1)} %get-tuple-element.107), channel_id=1, source_target_pairs={{0,16},{16,32},{32,48},{48,64},{64,80},{80,96},{96,112},{1,17},{17... | collective-permute-start | bytes 6152 | tf_op jit(solution)/shard_map/ppermute | solution.py:30
  108.7 11.4 %collective-permute-start.13 = (f32[2,256,1]{2,1,0:T(8,128)S(1)}, f32[2,256,1]{2,1,0:T(8,128)S(1)}, u32[]{:S(2)}, u32[]{:S(2)}) collective-permute-start(f32[2,256,1]{2,1,0:T(8,128)S(1)} %get-tuple-element.106), channel_id=1, source_target_pairs={{16,0},{32,16},{48,32},{64,48},{80,64},{96,80},{112,96},{17,1},{33... | collective-permute-start | bytes 6152 | tf_op jit(solution)/shard_map/ppermute | solution.py:32
  110.0 11.7 %collective-permute-start.12 = (f32[2,256,1]{2,1,0:T(8,128)S(1)}, f32[2,256,1]{2,1,0:T(8,128)S(1)}, u32[]{:S(2)}, u32[]{:S(2)}) collective-permute-start(f32[2,256,1]{2,1,0:T(8,128)S(1)} %get-tuple-element.105), channel_id=1, source_target_pairs={{0,16},{16,32},{32,48},{48,64},{64,80},{80,96},{96,112},{1,17},{17... | collective-permute-start | bytes 6152 | tf_op jit(solution)/shard_map/ppermute | solution.py:30
  145.5 10.7 %collective-permute-start.21 = (f32[2,256,1]{2,1,0:T(8,128)S(1)}, f32[2,256,1]{2,1,0:T(8,128)S(1)}, u32[]{:S(2)}, u32[]{:S(2)}) collective-permute-start(f32[2,256,1]{2,1,0:T(8,128)S(1)} %get-tuple-element.104), channel_id=1, source_target_pairs={{16,0},{32,16},{48,32},{64,48},{80,64},{96,80},{112,96},{17,1},{33... | collective-permute-start | bytes 6152 | tf_op jit(solution)/shard_map/ppermute | solution.py:32
  146.8 11.2 %collective-permute-start.20 = (f32[2,256,1]{2,1,0:T(8,128)S(1)}, f32[2,256,1]{2,1,0:T(8,128)S(1)}, u32[]{:S(2)}, u32[]{:S(2)}) collective-permute-start(f32[2,256,1]{2,1,0:T(8,128)S(1)} %get-tuple-element.103), channel_id=1, source_target_pairs={{0,16},{16,32},{32,48},{48,64},{64,80},{80,96},{96,112},{1,17},{17... | collective-permute-start | bytes 6152 | tf_op jit(solution)/shard_map/ppermute | solution.py:30
  166.0 11.6 %collective-permute-start.25 = (f32[2,256,1]{2,1,0:T(8,128)S(1)}, f32[2,256,1]{2,1,0:T(8,128)S(1)}, u32[]{:S(2)}, u32[]{:S(2)}) collective-permute-start(f32[2,256,1]{2,1,0:T(8,128)S(1)} %get-tuple-element.102), channel_id=1, source_target_pairs={{16,0},{32,16},{48,32},{64,48},{80,64},{96,80},{112,96},{17,1},{33... | collective-permute-start | bytes 6152 | tf_op jit(solution)/shard_map/ppermute | solution.py:32
  167.3 12.1 %collective-permute-start.24 = (f32[2,256,1]{2,1,0:T(8,128)S(1)}, f32[2,256,1]{2,1,0:T(8,128)S(1)}, u32[]{:S(2)}, u32[]{:S(2)}) collective-permute-start(f32[2,256,1]{2,1,0:T(8,128)S(1)} %get-tuple-element.101), channel_id=1, source_target_pairs={{0,16},{16,32},{32,48},{48,64},{64,80},{80,96},{96,112},{1,17},{17... | collective-permute-start | bytes 6152 | tf_op jit(solution)/shard_map/ppermute | solution.py:30
  187.5 9.6 %collective-permute-start.29 = (f32[256,1]{1,0:T(8,128)S(1)}, f32[256,1]{1,0:T(8,128)S(1)}, u32[]{:S(2)}, u32[]{:S(2)}) collective-permute-start(f32[256,1]{1,0:T(8,128)S(1)} %get-tuple-element.142), channel_id=1, source_target_pairs={{0,16},{16,32},{32,48},{48,64},{64,80},{80,96},{96,112},{1,17},{17... | collective-permute-start | bytes 3080 | tf_op jit(solution)/shard_map/ppermute | solution.py:30
  205.6 11.2 %collective-permute-start.33 = (f32[2,256,1]{2,1,0:T(8,128)S(1)}, f32[2,256,1]{2,1,0:T(8,128)S(1)}, u32[]{:S(2)}, u32[]{:S(2)}) collective-permute-start(f32[2,256,1]{2,1,0:T(8,128)S(1)} %get-tuple-element.100), channel_id=1, source_target_pairs={{16,0},{32,16},{48,32},{64,48},{80,64},{96,80},{112,96},{17,1},{33... | collective-permute-start | bytes 6152 | tf_op jit(solution)/shard_map/ppermute | solution.py:32
  206.9 11.6 %collective-permute-start.32 = (f32[2,256,1]{2,1,0:T(8,128)S(1)}, f32[2,256,1]{2,1,0:T(8,128)S(1)}, u32[]{:S(2)}, u32[]{:S(2)}) collective-permute-start(f32[2,256,1]{2,1,0:T(8,128)S(1)} %get-tuple-element.99), channel_id=1, source_target_pairs={{0,16},{16,32},{32,48},{48,64},{64,80},{80,96},{96,112},{1,17},{17... | collective-permute-start | bytes 6152 | tf_op jit(solution)/shard_map/ppermute | solution.py:30
  228.1 10.8 %collective-permute-start.37 = (f32[2,256,1]{2,1,0:T(8,128)S(1)}, f32[2,256,1]{2,1,0:T(8,128)S(1)}, u32[]{:S(2)}, u32[]{:S(2)}) collective-permute-start(f32[2,256,1]{2,1,0:T(8,128)S(1)} %get-tuple-element.98), channel_id=1, source_target_pairs={{16,0},{32,16},{48,32},{64,48},{80,64},{96,80},{112,96},{17,1},{33... | collective-permute-start | bytes 6152 | tf_op jit(solution)/shard_map/ppermute | solution.py:32
  229.4 11.0 %collective-permute-start.36 = (f32[2,256,1]{2,1,0:T(8,128)S(1)}, f32[2,256,1]{2,1,0:T(8,128)S(1)}, u32[]{:S(2)}, u32[]{:S(2)}) collective-permute-start(f32[2,256,1]{2,1,0:T(8,128)S(1)} %get-tuple-element.97), channel_id=1, source_target_pairs={{0,16},{16,32},{32,48},{48,64},{64,80},{80,96},{96,112},{1,17},{17... | collective-permute-start | bytes 6152 | tf_op jit(solution)/shard_map/ppermute | solution.py:30
  250.6 9.6 %collective-permute-start.41 = (f32[256,1]{1,0:T(8,128)S(1)}, f32[256,1]{1,0:T(8,128)S(1)}, u32[]{:S(2)}, u32[]{:S(2)}) collective-permute-start(f32[256,1]{1,0:T(8,128)S(1)} %get-tuple-element.140), channel_id=1, source_target_pairs={{0,16},{16,32},{32,48},{48,64},{64,80},{80,96},{96,112},{1,17},{17... | collective-permute-start | bytes 3080 | tf_op jit(solution)/shard_map/ppermute | solution.py:30
  269.7 11.2 %collective-permute-start.45 = (f32[2,256,1]{2,1,0:T(8,128)S(1)}, f32[2,256,1]{2,1,0:T(8,128)S(1)}, u32[]{:S(2)}, u32[]{:S(2)}) collective-permute-start(f32[2,256,1]{2,1,0:T(8,128)S(1)} %get-tuple-element.96), channel_id=1, source_target_pairs={{16,0},{32,16},{48,32},{64,48},{80,64},{96,80},{112,96},{17,1},{33... | collective-permute-start | bytes 6152 | tf_op jit(solution)/shard_map/ppermute | solution.py:32
  271.0 11.7 %collective-permute-start.44 = (f32[2,256,1]{2,1,0:T(8,128)S(1)}, f32[2,256,1]{2,1,0:T(8,128)S(1)}, u32[]{:S(2)}, u32[]{:S(2)}) collective-permute-start(f32[2,256,1]{2,1,0:T(8,128)S(1)} %get-tuple-element.95), channel_id=1, source_target_pairs={{0,16},{16,32},{32,48},{48,64},{64,80},{80,96},{96,112},{1,17},{17... | collective-permute-start | bytes 6152 | tf_op jit(solution)/shard_map/ppermute | solution.py:30
  294.1 11.3 %collective-permute-start.49 = (f32[2,256,1]{2,1,0:T(8,128)S(1)}, f32[2,256,1]{2,1,0:T(8,128)S(1)}, u32[]{:S(2)}, u32[]{:S(2)}) collective-permute-start(f32[2,256,1]{2,1,0:T(8,128)S(1)} %get-tuple-element.94), channel_id=1, source_target_pairs={{16,0},{32,16},{48,32},{64,48},{80,64},{96,80},{112,96},{17,1},{33... | collective-permute-start | bytes 6152 | tf_op jit(solution)/shard_map/ppermute | solution.py:32
  295.4 11.7 %collective-permute-start.48 = (f32[2,256,1]{2,1,0:T(8,128)S(1)}, f32[2,256,1]{2,1,0:T(8,128)S(1)}, u32[]{:S(2)}, u32[]{:S(2)}) collective-permute-start(f32[2,256,1]{2,1,0:T(8,128)S(1)} %get-tuple-element.93), channel_id=1, source_target_pairs={{0,16},{16,32},{32,48},{48,64},{64,80},{80,96},{96,112},{1,17},{17... | collective-permute-start | bytes 6152 | tf_op jit(solution)/shard_map/ppermute | solution.py:30
  316.5 11.7 %collective-permute-start.53 = (f32[2,256,1]{2,1,0:T(8,128)S(1)}, f32[2,256,1]{2,1,0:T(8,128)S(1)}, u32[]{:S(2)}, u32[]{:S(2)}) collective-permute-start(f32[2,256,1]{2,1,0:T(8,128)S(1)} %get-tuple-element.92), channel_id=1, source_target_pairs={{16,0},{32,16},{48,32},{64,48},{80,64},{96,80},{112,96},{17,1},{33... | collective-permute-start | bytes 6152 | tf_op jit(solution)/shard_map/ppermute | solution.py:32
  317.8 12.1 %collective-permute-start.52 = (f32[2,256,1]{2,1,0:T(8,128)S(1)}, f32[2,256,1]{2,1,0:T(8,128)S(1)}, u32[]{:S(2)}, u32[]{:S(2)}) collective-permute-start(f32[2,256,1]{2,1,0:T(8,128)S(1)} %get-tuple-element.91), channel_id=1, source_target_pairs={{0,16},{16,32},{32,48},{48,64},{64,80},{80,96},{96,112},{1,17},{17... | collective-permute-start | bytes 6152 | tf_op jit(solution)/shard_map/ppermute | solution.py:30
  338.9 10.5 %collective-permute-start.57 = (f32[2,256,1]{2,1,0:T(8,128)S(1)}, f32[2,256,1]{2,1,0:T(8,128)S(1)}, u32[]{:S(2)}, u32[]{:S(2)}) collective-permute-start(f32[2,256,1]{2,1,0:T(8,128)S(1)} %get-tuple-element.90), channel_id=1, source_target_pairs={{16,0},{32,16},{48,32},{64,48},{80,64},{96,80},{112,96},{17,1},{33... | collective-permute-start | bytes 6152 | tf_op jit(solution)/shard_map/ppermute | solution.py:32
  340.2 10.7 %collective-permute-start.56 = (f32[2,256,1]{2,1,0:T(8,128)S(1)}, f32[2,256,1]{2,1,0:T(8,128)S(1)}, u32[]{:S(2)}, u32[]{:S(2)}) collective-permute-start(f32[2,256,1]{2,1,0:T(8,128)S(1)} %get-tuple-element.89), channel_id=1, source_target_pairs={{0,16},{16,32},{32,48},{48,64},{64,80},{80,96},{96,112},{1,17},{17... | collective-permute-start | bytes 6152 | tf_op jit(solution)/shard_map/ppermute | solution.py:30
  361.7 10.8 %collective-permute-start.61 = (f32[2,256,1]{2,1,0:T(8,128)S(1)}, f32[2,256,1]{2,1,0:T(8,128)S(1)}, u32[]{:S(2)}, u32[]{:S(2)}) collective-permute-start(f32[2,256,1]{2,1,0:T(8,128)S(1)} %get-tuple-element.88), channel_id=1, source_target_pairs={{16,0},{32,16},{48,32},{64,48},{80,64},{96,80},{112,96},{17,1},{33... | collective-permute-start | bytes 6152 | tf_op jit(solution)/shard_map/ppermute | solution.py:32
  363.0 11.0 %collective-permute-start.60 = (f32[2,256,1]{2,1,0:T(8,128)S(1)}, f32[2,256,1]{2,1,0:T(8,128)S(1)}, u32[]{:S(2)}, u32[]{:S(2)}) collective-permute-start(f32[2,256,1]{2,1,0:T(8,128)S(1)} %get-tuple-element.87), channel_id=1, source_target_pairs={{0,16},{16,32},{32,48},{48,64},{64,80},{80,96},{96,112},{1,17},{17... | collective-permute-start | bytes 6152 | tf_op jit(solution)/shard_map/ppermute | solution.py:30
  374.1 9.8 %collective-permute-start.63 = (f32[2,1,258]{2,1,0:T(1,128)S(1)}, f32[2,1,258]{2,1,0:T(1,128)S(1)}, u32[]{:S(2)}, u32[]{:S(2)}) collective-permute-start(f32[2,1,258]{2,1,0:T(1,128)S(1)} %get-tuple-element.35), channel_id=1, source_target_pairs={{1,0},{2,1},{3,2},{4,3},{5,4},{6,5},{7,6},{8,7},{9,8},{10,9},{11,1... | collective-permute-start | bytes 6200 | tf_op jit(solution)/shard_map/ppermute | solution.py:32
  387.0 10.8 %collective-permute-start.65 = (f32[2,256,1]{2,1,0:T(8,128)S(1)}, f32[2,256,1]{2,1,0:T(8,128)S(1)}, u32[]{:S(2)}, u32[]{:S(2)}) collective-permute-start(f32[2,256,1]{2,1,0:T(8,128)S(1)} %get-tuple-element.86), channel_id=1, source_target_pairs={{16,0},{32,16},{48,32},{64,48},{80,64},{96,80},{112,96},{17,1},{33... | collective-permute-start | bytes 6152 | tf_op jit(solution)/shard_map/ppermute | solution.py:32
  388.3 11.0 %collective-permute-start.64 = (f32[2,256,1]{2,1,0:T(8,128)S(1)}, f32[2,256,1]{2,1,0:T(8,128)S(1)}, u32[]{:S(2)}, u32[]{:S(2)}) collective-permute-start(f32[2,256,1]{2,1,0:T(8,128)S(1)} %get-tuple-element.85), channel_id=1, source_target_pairs={{0,16},{16,32},{32,48},{48,64},{64,80},{80,96},{96,112},{1,17},{17... | collective-permute-start | bytes 6152 | tf_op jit(solution)/shard_map/ppermute | solution.py:30
  407.1 9.7 %collective-permute-start.67 = (f32[2,1,258]{2,1,0:T(1,128)S(1)}, f32[2,1,258]{2,1,0:T(1,128)S(1)}, u32[]{:S(2)}, u32[]{:S(2)}) collective-permute-start(f32[2,1,258]{2,1,0:T(1,128)S(1)} %get-tuple-element.33), channel_id=1, source_target_pairs={{1,0},{2,1},{3,2},{4,3},{5,4},{6,5},{7,6},{8,7},{9,8},{10,9},{11,1... | collective-permute-start | bytes 6200 | tf_op jit(solution)/shard_map/ppermute | solution.py:32
  (53 other events, 822.2 us)
Sparse Core Ops, SparseCore 0:
  14.8 49.5 all-gather.4
  434.5 189.2 all-reduce.2
